TPU v7x, 32 devices: a whole 2x2x4 slice. The times are simulated.
32 devices in a mesh: grp: 2 (over x), tm: 4 (over y, core), tile: 4 (over z).
Axes of the slice: x: 2, y: 2, z: 4, core: 2. Of those that a mesh axis runs over, the one named last changes fastest.
Arguments:
- frames: bfloat16 [64, 1024, 1024], P(('grp', 'tm'), 'tile'), parts along dimension 0, may hold values from -3 to 3
- inverse_taps: float32 [48], replicated, may hold values from -3 to 3
- mode_rate: float32 [1024, 1024], P(None, 'tile'), may hold values from 0.00625 to 0.2
- frame_factor: float32 [64], P(('grp', 'tm')), parts along dimension 0, may hold values from 0.5 to 1
Outputs:
- superheat: bfloat16 [64, 1024, 1024], P(('grp', 'tm'), 'tile'), parts along dimension 0
There are 2 independent parts, one for each index of `grp`. A program takes and returns all parts, laid end to end along the dimension named above; an argument that names none is the same for every part. Nothing has to cross between parts.
All inputs are finite; a program needn't handle non-finite values.
Results may differ from a plain program's by a relative error of at most 0.0097.
Values may be sent and summed in bfloat16 or wider, within the bound.
A program may use at most 128 MiB of HBM per device.

v0:
```python
import jax
import jax.numpy as jnp
from jax import lax
from jax.sharding import PartitionSpec as P


def from_behind(block, axis, distance):
    devices = range(lax.axis_size(axis))
    route = [(i - distance, i) for i in devices if i - distance in devices]
    return lax.ppermute(block, axis, route)


def cosine_matrix(points):
    freq_idx = jnp.arange(points, dtype=jnp.int32)[:, None]
    cell_idx = jnp.arange(points, dtype=jnp.int32)[None, :]
    phase = (2 * cell_idx + 1) * freq_idx % (4 * points)
    angle = jnp.pi * phase.astype(jnp.float32) / (2.0 * points)
    values = jnp.cos(angle) * jnp.sqrt(2.0 / points)
    values = jnp.where(freq_idx == 0, values / jnp.sqrt(2.0), values)
    return values.astype(jnp.bfloat16)


def on_device(frames, inverse_taps, mode_rate, frame_factor):
    segment_span, tile_rows, frame_side = frames.shape
    tap_count = inverse_taps.shape[0]
    basis = cosine_matrix(frame_side)
    taps_b = inverse_taps.astype(jnp.bfloat16).astype(jnp.float32)
    offset = (
        jnp.arange(segment_span)[:, None]
        + (tap_count - 1)
        - jnp.arange(segment_span + tap_count - 1)[None, :]
    )
    onehot = offset[:, :, None] == jnp.arange(tap_count)[None, None, :]
    toeplitz = jnp.sum(jnp.where(onehot, taps_b[None, None, :], 0.0), axis=2).astype(jnp.bfloat16)
    reach = (tap_count - 1 + segment_span - 1) // segment_span
    hop_count = min(reach, lax.axis_size("tm") - 1)
    received = []
    moving = frames
    for hop_index in range(hop_count):
        moving = from_behind(moving, "tm", 1)
        received.append(moving)
    missing = reach - hop_count
    pieces = []
    if missing > 0:
        pieces.append(jnp.zeros((missing * segment_span, tile_rows, frame_side), jnp.bfloat16))
    pieces = pieces + received[::-1]
    history_all = jnp.concatenate(pieces, axis=0)
    earlier = history_all[history_all.shape[0] - (tap_count - 1) :]
    joined = jnp.concatenate([earlier, frames], axis=0)
    wall_heat_flux = jnp.einsum("tj,jrw->trw", toeplitz, joined, preferred_element_type=jnp.float32)
    wall_heat_flux = wall_heat_flux.astype(jnp.bfloat16)
    spectra = jnp.einsum(
        "kr,frc->fkc",
        basis,
        lax.all_to_all(
            jnp.einsum(
                "frw,kw->frk", wall_heat_flux, basis, preferred_element_type=jnp.float32
            ).astype(jnp.bfloat16),
            "tile",
            split_axis=2,
            concat_axis=1,
            tiled=True,
        ),
        preferred_element_type=jnp.float32,
    )
    retain = jnp.exp(-mode_rate)

    def advance(held, inputs):
        decay, running = held
        spectrum, factor = inputs
        rate_now = retain * factor
        decay = rate_now * decay
        running = rate_now * running + spectrum
        return ((decay, running), (decay, running))

    start_decay = jnp.ones_like(retain)
    start_state = jnp.zeros_like(retain)
    (last_decay, last_state), (decays, partial_value) = lax.scan(
        advance, (start_decay, start_state), (spectra, frame_factor)
    )

    def turn(round_number, incoming):
        return from_behind(last_decay * incoming + last_state, "tm", 1)

    carried = lax.fori_loop(0, lax.axis_size("tm") - 1, turn, start_state)
    running_b = (partial_value + decays * carried[None]).astype(jnp.bfloat16)
    return jnp.einsum(
        "frk,kw->frw",
        lax.all_to_all(
            jnp.einsum("kr,fkc->frc", basis, running_b, preferred_element_type=jnp.float32).astype(
                jnp.bfloat16
            ),
            "tile",
            split_axis=1,
            concat_axis=2,
            tiled=True,
        ),
        basis,
        preferred_element_type=jnp.float32,
    ).astype(jnp.bfloat16)


def solution(mesh):
    return jax.shard_map(
        on_device,
        mesh=mesh,
        in_specs=(P(("grp", "tm"), "tile", None), P(), P(None, "tile"), P(("grp", "tm"))),
        out_specs=P(("grp", "tm"), "tile", None),
        check_vma=False,
    )
```

profile of v0, /device:TPU:1, one launch (start us, length us, event | category | flops | bytes accessed | tf_op | source)
XLA Modules:
  0.0 596.6 jit_solution(18411087734227628912)
XLA Ops:
  0.0 4.5 copy.15
  4.5 4.5 collective-permute-start.1
  9.1 45.4 %collective-permute-done.1 = bf16[8,256,1024]{2,0,1:T(8,128)(2,1)S(1)} collective-permute-done((bf16[8,256,1024]{2,0,1:T(8,128)(2,1)S(1)}, bf16[8,256,1024]{2,0,1:T(8,128)(2,1)S(1)}, u32[]{:S(2)}, u32[]{:S(2)}) %collective-permute-start.1) | collective-permute-done | bytes 4194336 | tf_op jit(solution)/shard_map/ppermute | solution.py:10
  54.5 4.4 collective-permute-start.2
  58.9 45.4 %collective-permute-done.2 = bf16[8,256,1024]{2,0,1:T(8,128)(2,1)S(1)} collective-permute-done((bf16[8,256,1024]{2,0,1:T(8,128)(2,1)S(1)}, bf16[8,256,1024]{2,0,1:T(8,128)(2,1)S(1)}, u32[]{:S(2)}, u32[]{:S(2)}) %collective-permute-start.2) | collective-permute-done | bytes 4194336 | tf_op jit(solution)/shard_map/ppermute | solution.py:10
  104.3 4.4 collective-permute-start.3
  109.0 45.1 %collective-permute-done.3 = bf16[8,256,1024]{2,0,1:T(8,128)(2,1)S(1)} collective-permute-done((bf16[8,256,1024]{2,0,1:T(8,128)(2,1)S(1)}, bf16[8,256,1024]{2,0,1:T(8,128)(2,1)S(1)}, u32[]{:S(2)}, u32[]{:S(2)}) %collective-permute-start.3) | collective-permute-done | bytes 4194336 | tf_op jit(solution)/shard_map/ppermute | solution.py:10
  154.1 14.9 %pad_maximum_fusion = bf16[47,256,1024]{2,0,1:T(8,128)(2,1)} fusion(bf16[8,256,1024]{2,0,1:T(8,128)(2,1)S(1)} %collective-permute-done.1, bf16[8,256,1024]{2,0,1:T(8,128)(2,1)S(1)} %collective-permute-done.2, bf16[8,256,1024]{2,0,1:T(8,128)(2,1)S(1)} %collective-permute-done.3, bf16[47]{0:T(256)(128)(2,1)S(1)} %pad_slice_fusion), kind=kLoop, calls=%fused_computation.11 | loop fusion | flops 98566144 | bytes 37224544 | tf_op jit(solution)/shard_map/concatenate | solution.py:47
  169.0 14.9 %fusion.18 = bf16[8,256,1024]{2,0,1:T(8,128)(2,1)} fusion(bf16[8,256,1024]{2,0,1:T(8,128)(2,1)} %copy-done, bf16[47,256,1024]{2,0,1:T(8,128)(2,1)} %pad_maximum_fusion, bf16[8,55]{1,0:T(8,128)(2,1)S(1)} %select_reduce_fusion), kind=kOutput, calls=%fused_computation.35 | convolution fusion | flops 290455552 | bytes 33031024 | tf_op jit(solution)/shard_map/tj,jrw->trw/dot_general | solution.py:50
  183.9 30.2 %fusion.15 = bf16[8,256,1024]{2,1,0:T(8,128)(2,1)} fusion(bf16[8,256,1024]{2,0,1:T(8,128)(2,1)} %fusion.18, s32[1024]{0:T(1024)S(1)} %multiply_add_fusion.1, pred[1024]{0:T(1024)(128)(4,1)S(1)} %iota_compare_fusion.1), kind=kOutput, calls=%fused_computation.34 | convolution fusion | flops 4315938816 | bytes 8393728 | tf_op jit(solution)/shard_map/frw,kw->frk/dot_general | solution.py:56
  214.1 7.0 %copy.18 = bf16[8,256,1024]{1,0,2:T(8,128)(2,1)} copy(bf16[8,256,1024]{2,1,0:T(8,128)(2,1)} %fusion.15) | data formatting | bytes 8388608 | tf_op jit(solution)/shard_map/convert_element_type | solution.py:58
  221.1 5.0 all-to-all-start
  227.4 52.1 %all-to-all-done = bf16[8,256,1024]{1,0,2:T(8,128)(2,1)} async-done(((bf16[8,256,1024]{1,0,2:T(8,128)(2,1)}), bf16[8,256,1024]{1,0,2:T(8,128)(2,1)}, u32[]{:S(2)}, u32[]{:S(2)}) %all-to-all-start) | async-done | bytes 4194336 | tf_op jit(solution)/shard_map/all_to_all | solution.py:55
  279.5 7.4 %copy.33 = bf16[8,256,4,256]{1,2,3,0:T(4,128)(2,1)} copy(bf16[8,256,4,256]{1,0,3,2:T(8,128)(2,1)} %bitcast.2) | data formatting | bytes 8388608 | tf_op jit(solution)/shard_map/all_to_all | solution.py:55
  286.9 7.8 %all_to_all.29 = bf16[8,1024,256]{1,2,0:T(8,128)(2,1)} reshape(bf16[8,4,256,256]{2,1,3,0:T(4,128)(2,1)} %bitcast.37) | data formatting | bytes 8388608 | tf_op jit(solution)/shard_map/all_to_all | solution.py:55
  294.7 23.9 %convolution_bitcast_fusion = f32[8,1024,256]{1,2,0:T(8,128)} fusion(bf16[8,1024,256]{1,2,0:T(8,128)(2,1)} %all_to_all.29, s32[1024]{0:T(1024)S(1)} %multiply_add_fusion.1, pred[1024]{0:T(1024)(128)(4,1)S(1)} %iota_compare_fusion.1), kind=kOutput, calls=%fused_computation.33 | convolution fusion | flops 4313841664 | bytes 12588032 | tf_op jit(solution)/shard_map/kr,frc->fkc/dot_general | solution.py:52
  318.6 69.1 %while.28 = (s32[]{:T(128)}, f32[1024,256]{1,0:T(8,128)S(1)}, f32[1024,256]{1,0:T(8,128)S(1)}, f32[8,1024,256]{2,1,0:T(8,128)}, f32[8,1024,256]{2,1,0:T(8,128)},...) while((s32[]{:T(128)}, f32[1024,256]{1,0:T(8,128)S(1)}, ...), condition=%wide.region_2.3_spmd.clone, body=%wide.region_1.2_spmd.clone.sunk | while | flops 1572867 | bytes 12584063 | solution.py:78
  323.0 4.2 bitcast_dynamic-update-slice_fusion.3
  340.3 4.2 bitcast_dynamic-update-slice_fusion.3
  357.6 4.2 bitcast_dynamic-update-slice_fusion.3
  387.7 52.3 %while.27 = (s32[]{:T(128)}, f32[1024,256]{1,0:T(8,128)S(1)}, f32[1024,256]{1,0:T(8,128)S(1)}, f32[1024,256]{1,0:T(8,128)S(1)}, s32[]{:T(128)}) while((s32[]{:T(128)}, f32[1024,256]{1,0:T(8,128)S(1)}, f32[1024,256]{1,0:T(8,128)S(1)}, f32[1024,256]{1,0:T(8,128)S(1)}, s32[]{:T(128)}) %tuple.47), condition=%wide.region_4.5_spmd, body=%wide.region_3.4_spmd.sunk | while | flops 524290 | bytes 8388709 | solution.py:85
  392.8 12.0 %collective-permute-done = f32[1024,256]{1,0:T(8,128)S(1)} collective-permute-done((f32[1024,256]{1,0:T(8,128)}, f32[1024,256]{1,0:T(8,128)S(1)}, u32[]{:S(2)}, u32[]{:S(2)}) %collective-permute-start) | collective-permute-done | bytes 1048608 | tf_op jit(solution)/shard_map/while/body/eval_jaxpr/ppermute | solution.py:10
  406.0 4.3 collective-permute-start
  410.3 12.0 %collective-permute-done = f32[1024,256]{1,0:T(8,128)S(1)} collective-permute-done((f32[1024,256]{1,0:T(8,128)}, f32[1024,256]{1,0:T(8,128)S(1)}, u32[]{:S(2)}, u32[]{:S(2)}) %collective-permute-start) | collective-permute-done | bytes 1048608 | tf_op jit(solution)/shard_map/while/body/eval_jaxpr/ppermute | solution.py:10
  423.5 4.3 collective-permute-start
  427.8 12.0 %collective-permute-done = f32[1024,256]{1,0:T(8,128)S(1)} collective-permute-done((f32[1024,256]{1,0:T(8,128)}, f32[1024,256]{1,0:T(8,128)S(1)}, u32[]{:S(2)}, u32[]{:S(2)}) %collective-permute-start) | collective-permute-done | bytes 1048608 | tf_op jit(solution)/shard_map/while/body/eval_jaxpr/ppermute | solution.py:10
  440.0 27.7 %convert_bitcast_fusion = bf16[8,1024,256]{1,2,0:T(8,128)(2,1)} fusion(f32[8,1024,256]{2,1,0:T(8,128)} %get-tuple-element.72, f32[8,1024,256]{2,1,0:T(8,128)} %get-tuple-element.73, f32[1024,256]{1,0:T(8,128)S(1)} %get-tuple-element.76, s32[1024]{0:T(1024)S(1)} %multiply_add_fusion.1, pred[1024]{0:T(1024)(128)(4,1)S(1)} %iota_compare_fusion.1), kind=kOutput, calls=%fused_computation.27 | convolution fusion | flops 4322230272 | bytes 22025216 | tf_op jit(solution)/shard_map/kr,fkc->frc/dot_general | solution.py:90
  467.6 6.9 %copy.22 = bf16[8,1024,256]{2,0,1:T(8,128)(2,1)} copy(bf16[8,1024,256]{1,2,0:T(8,128)(2,1)} %convert_bitcast_fusion) | data formatting | bytes 8388608 | tf_op jit(solution)/shard_map/convert_element_type | solution.py:90
  474.6 86.2 %all_to_all.36 = bf16[8,1024,256]{2,0,1:T(8,128)(2,1)S(1)} all-to-all(bf16[8,1024,256]{2,0,1:T(8,128)(2,1)} %copy.22), channel_id=1, replica_groups=mesh['grp'=2,'tm'=4,'tile'=4] {'tile'}, dimensions={1} | all-to-all | bytes 8388608 | tf_op jit(solution)/shard_map/all_to_all | solution.py:89
  560.7 5.2 copy.32
  566.0 7.7 %all_to_all.33 = bf16[8,256,1024]{2,1,0:T(8,128)(2,1)} reshape(bf16[8,256,4,256]{3,2,1,0:T(4,128)(2,1)} %bitcast.39) | data formatting | bytes 8388608 | tf_op jit(solution)/shard_map/all_to_all | solution.py:89
  573.7 22.5 %convolution_convert_fusion = bf16[8,256,1024]{2,1,0:T(8,128)(2,1)} fusion(bf16[8,256,1024]{2,1,0:T(8,128)(2,1)} %all_to_all.33, s32[1024]{0:T(1024)S(1)} %multiply_add_fusion.1, pred[1024]{0:T(1024)(128)(4,1)S(1)} %iota_compare_fusion.1), kind=kOutput, calls=%fused_computation.36 | convolution fusion | flops 4315938816 | bytes 8393728 | tf_op jit(solution)/shard_map/frk,kw->frw/dot_general | solution.py:87
  (55 shorter events, 65.3 us)
Async XLA Ops:
  0.0 108.8 %copy-start.2 = (f32[48]{0:T(128)S(1)}, f32[48]{0:T(128)}, u32[]{:S(2)}) copy-start(f32[48]{0:T(128)} %param.9) | copy-start | bytes 580
  4.5 149.6 %copy-start = (bf16[8,256,1024]{2,0,1:T(8,128)(2,1)}, bf16[8,256,1024]{2,0,1:T(8,128)(2,1)S(1)}, u32[]{:S(2)}) copy-start(bf16[8,256,1024]{2,0,1:T(8,128)(2,1)S(1)} %copy.15) | copy-start | bytes 12582916
  4.5 50.0 %collective-permute-start.1 = (bf16[8,256,1024]{2,0,1:T(8,128)(2,1)S(1)}, bf16[8,256,1024]{2,0,1:T(8,128)(2,1)S(1)}, u32[]{:S(2)}, u32[]{:S(2)}) collective-permute-start(bf16[8,256,1024]{2,0,1:T(8,128)(2,1)S(1)} %copy.15), channel_id=1, source_target_pairs={{0,4},{4,8},{8,12},{1,5},{5,9},{9,13},{2,6},{6,10},{10,14},{3,7},{... | collective-permute-start | bytes 12582920 | tf_op jit(solution)/shard_map/ppermute | solution.py:10
  54.5 49.8 %collective-permute-start.2 = (bf16[8,256,1024]{2,0,1:T(8,128)(2,1)S(1)}, bf16[8,256,1024]{2,0,1:T(8,128)(2,1)S(1)}, u32[]{:S(2)}, u32[]{:S(2)}) collective-permute-start(bf16[8,256,1024]{2,0,1:T(8,128)(2,1)S(1)} %collective-permute-done.1), channel_id=1, source_target_pairs={{0,4},{4,8},{8,12},{1,5},{5,9},{9,13},{2,6},{6,10},{10,14},{3,7},{... | collective-permute-start | bytes 12582920 | tf_op jit(solution)/shard_map/ppermute | solution.py:10
  104.3 49.8 %collective-permute-start.3 = (bf16[8,256,1024]{2,0,1:T(8,128)(2,1)S(1)}, bf16[8,256,1024]{2,0,1:T(8,128)(2,1)S(1)}, u32[]{:S(2)}, u32[]{:S(2)}) collective-permute-start(bf16[8,256,1024]{2,0,1:T(8,128)(2,1)S(1)} %collective-permute-done.2), channel_id=1, source_target_pairs={{0,4},{4,8},{8,12},{1,5},{5,9},{9,13},{2,6},{6,10},{10,14},{3,7},{... | collective-permute-start | bytes 12582920 | tf_op jit(solution)/shard_map/ppermute | solution.py:10
  221.1 5.0 copy-start.1
  221.1 58.3 %all-to-all-start = ((bf16[8,256,1024]{1,0,2:T(8,128)(2,1)}), bf16[8,256,1024]{1,0,2:T(8,128)(2,1)}, u32[]{:S(2)}, u32[]{:S(2)}) async-start(bf16[8,256,1024]{1,0,2:T(8,128)(2,1)} %copy.18), calls=%async_computation | async-start | bytes 8388608 | tf_op jit(solution)/shard_map/all_to_all | solution.py:55
  294.7 23.9 %copy-start.3 = (f32[8]{0:T(128)S(1)}, f32[8]{0:T(128)}, u32[]{:S(2)}) copy-start(f32[8]{0:T(128)} %param.11) | copy-start | bytes 100
  388.9 15.9 %collective-permute-start = (f32[1024,256]{1,0:T(8,128)}, f32[1024,256]{1,0:T(8,128)S(1)}, u32[]{:S(2)}, u32[]{:S(2)}) collective-permute-start(f32[1024,256]{1,0:T(8,128)} %multiply_add_fusion.3), channel_id=1, source_target_pairs={{0,4},{4,8},{8,12},{1,5},{5,9},{9,13},{2,6},{6,10},{10,14},{3,7},{... | collective-permute-start | bytes 3145736 | tf_op jit(solution)/shard_map/while/body/eval_jaxpr/ppermute | solution.py:10
  406.0 16.3 %collective-permute-start = (f32[1024,256]{1,0:T(8,128)}, f32[1024,256]{1,0:T(8,128)S(1)}, u32[]{:S(2)}, u32[]{:S(2)}) collective-permute-start(f32[1024,256]{1,0:T(8,128)} %multiply_add_fusion.3), channel_id=1, source_target_pairs={{0,4},{4,8},{8,12},{1,5},{5,9},{9,13},{2,6},{6,10},{10,14},{3,7},{... | collective-permute-start | bytes 3145736 | tf_op jit(solution)/shard_map/while/body/eval_jaxpr/ppermute | solution.py:10
  423.5 16.3 %collective-permute-start = (f32[1024,256]{1,0:T(8,128)}, f32[1024,256]{1,0:T(8,128)S(1)}, u32[]{:S(2)}, u32[]{:S(2)}) collective-permute-start(f32[1024,256]{1,0:T(8,128)} %multiply_add_fusion.3), channel_id=1, source_target_pairs={{0,4},{4,8},{8,12},{1,5},{5,9},{9,13},{2,6},{6,10},{10,14},{3,7},{... | collective-permute-start | bytes 3145736 | tf_op jit(solution)/shard_map/while/body/eval_jaxpr/ppermute | solution.py:10
where the time goes:
time: 605 us; the launch traced here: 597 us
  waiting for transfers between devices  224 us (37%)
  matrix products  119 us (20%)
  blocking collectives  86.2 us (14%)
  local copies, waits for them, and re-layouts  82.4 us (14%)
  other arithmetic  53.2 us (9%)
  starting transfers between devices  30.7 us (5%)
    ppermute x6, waiting for transfers between devices, from_behind(): return lax.ppermute(block, axis, route)  172 us
    all_to_all x1, blocking collectives, on_device(): lax.all_to_all(jnp.einsum('kr,fkc->frc', basis, running_b, preferred_elem...  86.2 us
    all_to_all x1, waiting for transfers between devices, on_device(): lax.all_to_all(jnp.einsum('frw,kw->frk', wall_heat_flux, basis, preferred...  52.1 us
    dynamic_slice x24, local copies, waits for them, and re-layouts, on_device(): lax.scan(advance, (start_decay, start_state), (spectra, frame_factor))  35.6 us
    dynamic_update_slice x8, other arithmetic, on_device(): lax.scan(advance, (start_decay, start_state), (spectra, frame_factor))  33.4 us
    dot_general x1, matrix products, on_device(): jnp.einsum('frw,kw->frk', wall_heat_flux, basis, preferred_element_type=j...  30.2 us
    dot_general x1, matrix products, on_device(): jnp.einsum('kr,fkc->frc', basis, running_b, preferred_element_type=jnp.fl...  27.7 us
    ppermute x6, starting transfers between devices, from_behind(): return lax.ppermute(block, axis, route)  25.7 us
  transfers between devices with their start and end apart: 7, of which 7 were waited for; matrix products, arithmetic and copies ran while one was open for 0% of the time, Pallas kernels for 0%

commit v1 on v0

v1 whole, which is shorter than its diff:
```python
import functools

import jax
import jax.numpy as jnp
from jax import lax
from jax.experimental import pallas as pl
from jax.experimental.pallas import tpu as pltpu
from jax.sharding import PartitionSpec as P

MESH = pl.DeviceIdType.MESH
GROUP = 16
PIECE = 64
CARRY_PIECES = 4


def cosine_values(freq_idx, cell_idx, points):
    phase = (2 * cell_idx + 1) * freq_idx % (4 * points)
    angle = jnp.pi * phase.astype(jnp.float32) / (2.0 * points)
    values = jnp.cos(angle) * jnp.sqrt(2.0 / points)
    values = jnp.where(freq_idx == 0, values / jnp.sqrt(2.0), values)
    return values.astype(jnp.bfloat16)


def dot(a, b):
    return jnp.dot(a, b, preferred_element_type=jnp.float32)


def kernel(
    x_hbm, taps, rate_hbm, factor, bt_hbm, bp_hbm, out_hbm,
    x, hist, bt, bp, retain, flux, send1, colp, acc, tk, carry, cout, dec, rb, send2, rowp, outv,
    load_sem, hist_send, hist_recv, fwd_send, fwd_recv, carry_send, carry_recv,
    inv_send, inv_recv, out_sem,
):
    span, rows, side = x.shape
    hops = hist.shape[0]
    pieces, _, depth, cols = colp.shape
    tap_count = taps.shape[0]
    tiles = side // rows
    times = lax.axis_size("tm")
    j = lax.axis_index("tm")
    z = lax.axis_index("tile")

    def partner(d):
        return lax.rem(z + d, tiles)

    def source(d):
        return lax.rem(z + tiles - d, tiles)

    loads = [
        pltpu.make_async_copy(src, dst, load_sem.at[n])
        for n, (src, dst) in enumerate(((x_hbm, x), (bt_hbm, bt), (bp_hbm, bp), (rate_hbm, retain)))
    ]
    for load in loads:
        load.start()

    barrier = pltpu.get_barrier_semaphore()
    for d in range(1, tiles):
        pl.semaphore_signal(barrier, inc=1, device_id={"tile": partner(d)}, device_id_type=MESH)

    for other in (lax.rem(j + 1, times), lax.rem(j + times - 1, times)):
        pl.semaphore_signal(barrier, inc=1, device_id={"tm": other}, device_id_type=MESH)

    pl.semaphore_wait(barrier, tiles + 1)

    def piece_rows(i):
        return pl.ds(pl.multiple_of(i * PIECE, PIECE), PIECE)

    def hist_copy(h, i):
        src = x_hbm if h == 0 else hist.at[h - 1]
        return pltpu.make_async_remote_copy(
            src_ref=src.at[:, piece_rows(i), :],
            dst_ref=hist.at[h, :, piece_rows(i), :],
            send_sem=hist_send.at[h, i],
            recv_sem=hist_recv.at[h, i],
            device_id={"tm": lax.rem(j + 1, times)},
            device_id_type=MESH,
        )

    def sends(h):
        return jnp.logical_and(j < times - 1, j >= h)

    def fwd_copy(i, d):
        return pltpu.make_async_remote_copy(
            src_ref=send1.at[i, d - 1],
            dst_ref=colp.at[i, :, pl.ds(pl.multiple_of(z * PIECE, PIECE), PIECE), :],
            send_sem=fwd_send.at[i, d - 1],
            recv_sem=fwd_recv.at[i, d - 1],
            device_id={"tile": partner(d)},
            device_id_type=MESH,
        )

    def fwd_arrival(i, d):
        return pltpu.make_async_remote_copy(
            src_ref=send1.at[i, d - 1],
            dst_ref=colp.at[i, :, pl.ds(pl.multiple_of(source(d) * PIECE, PIECE), PIECE), :],
            send_sem=fwd_send.at[i, d - 1],
            recv_sem=fwd_recv.at[i, d - 1],
            device_id={"tile": partner(d)},
            device_id_type=MESH,
        )

    @pl.when(sends(0))
    def _():
        hist_copy(0, 0).start()

    wide = (hops + 1) * span * GROUP
    out_pos = lax.broadcasted_iota(jnp.int32, (span * GROUP, wide), 0)
    in_pos = lax.broadcasted_iota(jnp.int32, (span * GROUP, wide), 1)
    lag = out_pos // GROUP + hops * span - in_pos // GROUP
    lag = jnp.where(out_pos % GROUP == in_pos % GROUP, lag, -1)
    tk[...] = lag.astype(jnp.float32)

    def tap_rows(n, _):
        here = pl.ds(pl.multiple_of(n * GROUP, GROUP), GROUP)
        lags = tk[here, :]
        values = jnp.zeros_like(lags)
        for k in range(tap_count):
            values = jnp.where(lags == float(k), taps[k], values)
        tk[here, :] = values
        return 0

    lax.fori_loop(0, span, tap_rows, 0)

    for h in range(hops):

        @pl.when(j <= h)
        def _(h=h):
            def clear(s, _):
                hist[h, s] = jnp.zeros((rows, side), hist.dtype)
                return 0

            lax.fori_loop(0, span, clear, 0)

    def clear_acc(s, _):
        acc[s] = jnp.zeros((side, cols), jnp.float32)
        return 0

    lax.fori_loop(0, span, clear_acc, 0)

    for load in loads:
        load.wait()

    def row_transform(i):
        for d in range(1, tiles):
            fwd_arrival(i, d).wait_recv()

        def frame(s, _):
            block = colp[i, s]
            for m in range(side // 256):
                here = slice(m * 256, (m + 1) * 256)
                basis = bp[here, pl.ds(pl.multiple_of(i * depth, depth), depth)]
                acc[s, here, :] += dot(basis, block)
            return 0

        lax.fori_loop(0, span, frame, 0)

    def forward(i, _):
        for h in range(hops):

            @pl.when(j > h)
            def _(h=h):
                hist_copy(h, i).wait_recv()

            if h + 1 < hops:

                @pl.when(sends(h + 1))
                def _(h=h):
                    hist_copy(h + 1, i).start()

        @pl.when(jnp.logical_and(sends(0), i < pieces - 1))
        def _():
            hist_copy(0, i + 1).start()

        matrix = tk[...].astype(jnp.bfloat16)

        def group(n, _):
            here = pl.ds(pl.multiple_of(i * PIECE + n * GROUP, GROUP), GROUP)
            blocks = [hist[h, :, here, :].reshape(span * GROUP, side) for h in reversed(range(hops))]
            blocks.append(x[:, here, :].reshape(span * GROUP, side))
            result = dot(matrix, jnp.concatenate(blocks, axis=0)).astype(jnp.bfloat16)
            flux[:, pl.ds(pl.multiple_of(n * GROUP, GROUP), GROUP), :] = result.reshape(span, GROUP, side)
            return 0

        lax.fori_loop(0, PIECE // GROUP, group, 0)

        for d in list(range(1, tiles)) + [0]:
            modes = pl.ds(pl.multiple_of(partner(d) * cols, cols), cols)
            result = dot(flux[...].reshape(span * PIECE, side), bt[:, modes]).astype(jnp.bfloat16)
            result = result.reshape(span, PIECE, cols)
            if d == 0:
                colp[i, :, pl.ds(pl.multiple_of(z * PIECE, PIECE), PIECE), :] = result
            else:
                send1[i, d - 1] = result
                fwd_copy(i, d).start()

        @pl.when(i > 0)
        def _():
            row_transform(i - 1)

        return 0

    def decay(n, _):
        here = pl.ds(pl.multiple_of(n * 64, 64), 64)
        retain[here, :] = jnp.exp(-retain[here, :])
        return 0

    lax.fori_loop(0, side // 64, decay, 0)
    lax.fori_loop(0, pieces, forward, 0)
    row_transform(pieces - 1)

    def close(n, _):
        here = pl.ds(pl.multiple_of(n * 64, 64), 64)
        rate = retain[here, :]
        last = acc[0, here, :]
        whole = rate * factor[0]
        for s in range(1, span):
            now = rate * factor[s]
            last = now * last + acc[s, here, :]
            whole = now * whole
        cout[here, :] = last
        dec[here, :] = whole
        return 0

    lax.fori_loop(0, side // 64, close, 0)

    share = side // CARRY_PIECES

    def carry_copy(q):
        here = pl.ds(q * share, share)
        return pltpu.make_async_remote_copy(
            src_ref=cout.at[here, :],
            dst_ref=carry.at[here, :],
            send_sem=carry_send.at[q],
            recv_sem=carry_recv.at[q],
            device_id={"tm": lax.rem(j + 1, times)},
            device_id_type=MESH,
        )

    @pl.when(j == 0)
    def _():
        carry[...] = jnp.zeros_like(carry)

    for q in range(CARRY_PIECES):

        @pl.when(j > 0)
        def _(q=q):
            carry_copy(q).wait_recv()
            here = pl.ds(q * share, share)
            cout[here, :] = dec[here, :] * carry[here, :] + cout[here, :]

        @pl.when(j < times - 1)
        def _(q=q):
            carry_copy(q).start()

    def inv_copy(s, d):
        return pltpu.make_async_remote_copy(
            src_ref=send2.at[s, d - 1],
            dst_ref=rowp.at[s, :, pl.ds(pl.multiple_of(z * cols, cols), cols)],
            send_sem=inv_send.at[s, d - 1],
            recv_sem=inv_recv.at[s, d - 1],
            device_id={"tile": partner(d)},
            device_id_type=MESH,
        )

    def inv_arrival(s, d):
        return pltpu.make_async_remote_copy(
            src_ref=send2.at[s, d - 1],
            dst_ref=rowp.at[s, :, pl.ds(pl.multiple_of(source(d) * cols, cols), cols)],
            send_sem=inv_send.at[s, d - 1],
            recv_sem=inv_recv.at[s, d - 1],
            device_id={"tile": partner(d)},
            device_id_type=MESH,
        )

    def inverse(s, _):
        fact = factor[s]

        def advance(n, _):
            here = pl.ds(pl.multiple_of(n * 128, 128), 128)
            now = (retain[here, :] * fact) * carry[here, :] + acc[s, here, :]
            carry[here, :] = now
            rb[here, :] = now.astype(jnp.bfloat16)
            return 0

        lax.fori_loop(0, side // 128, advance, 0)
        for d in list(range(1, tiles)) + [0]:
            mine = pl.ds(pl.multiple_of(partner(d) * rows, rows), rows)
            result = dot(bt[mine, :], rb[...]).astype(jnp.bfloat16)
            if d == 0:
                rowp[s, :, pl.ds(pl.multiple_of(z * cols, cols), cols)] = result
            else:
                send2[s, d - 1] = result
                inv_copy(s, d).start()
        return 0

    lax.fori_loop(0, span, inverse, 0)

    def finish(s, _):
        for d in range(1, tiles):
            inv_arrival(s, d).wait_recv()
        outv[s] = lax.dot_general(
            rowp[s], bt[...], (((1,), (1,)), ((), ())), preferred_element_type=jnp.float32
        ).astype(jnp.bfloat16)
        pltpu.make_async_copy(outv.at[s], out_hbm.at[s], out_sem.at[s]).start()
        return 0

    lax.fori_loop(0, span, finish, 0)

    def drain_frames(s, _):
        for d in range(1, tiles):
            inv_copy(s, d).wait_send()
        pltpu.make_async_copy(outv.at[s], out_hbm.at[s], out_sem.at[s]).wait()
        return 0

    lax.fori_loop(0, span, drain_frames, 0)

    def drain_pieces(i, _):
        for d in range(1, tiles):
            fwd_copy(i, d).wait_send()
        for h in range(hops):

            @pl.when(sends(h))
            def _(h=h):
                hist_copy(h, i).wait_send()

        return 0

    lax.fori_loop(0, pieces, drain_pieces, 0)

    @pl.when(j < times - 1)
    def _():
        for q in range(CARRY_PIECES):
            carry_copy(q).wait_send()


def on_device(frames, inverse_taps, mode_rate, frame_factor):
    span, rows, side = frames.shape
    tap_count = inverse_taps.shape[0]
    tiles = side // rows
    cols = side // tiles
    pieces = rows // PIECE
    depth = tiles * PIECE
    hops = min((tap_count - 1 + span - 1) // span, lax.axis_size("tm") - 1)
    index = jnp.arange(side, dtype=jnp.int32)
    place = index % depth
    cell = place // PIECE * rows + index // depth * PIECE + place % PIECE
    bt = cosine_values(index[None, :], index[:, None], side)
    bp = cosine_values(index[:, None], cell[None, :], side)
    any_space = pl.BlockSpec(memory_space=pl.ANY)
    smem = pl.BlockSpec(memory_space=pltpu.SMEM)
    b16, f32 = jnp.bfloat16, jnp.float32
    dma = pltpu.SemaphoreType.DMA
    return pl.pallas_call(
        kernel,
        out_shape=jax.ShapeDtypeStruct(frames.shape, b16),
        in_specs=[any_space, smem, any_space, smem, any_space, any_space],
        out_specs=any_space,
        scratch_shapes=[
            pltpu.VMEM((span, rows, side), b16),
            pltpu.VMEM((hops, span, rows, side), b16),
            pltpu.VMEM((side, side), b16),
            pltpu.VMEM((side, side), b16),
            pltpu.VMEM((side, cols), f32),
            pltpu.VMEM((span, PIECE, side), b16),
            pltpu.VMEM((pieces, tiles - 1, span, PIECE, cols), b16),
            pltpu.VMEM((pieces, span, depth, cols), b16),
            pltpu.VMEM((span, side, cols), f32),
            pltpu.VMEM((span * GROUP, (hops + 1) * span * GROUP), f32),
            pltpu.VMEM((side, cols), f32),
            pltpu.VMEM((side, cols), f32),
            pltpu.VMEM((side, cols), f32),
            pltpu.VMEM((side, cols), b16),
            pltpu.VMEM((span, tiles - 1, rows, cols), b16),
            pltpu.VMEM((span, rows, side), b16),
            pltpu.VMEM((span, rows, side), b16),
            dma((4,)),
            dma((hops, pieces)),
            dma((hops, pieces)),
            dma((pieces, tiles - 1)),
            dma((pieces, tiles - 1)),
            dma((CARRY_PIECES,)),
            dma((CARRY_PIECES,)),
            dma((span, tiles - 1)),
            dma((span, tiles - 1)),
            dma((span,)),
        ],
        compiler_params=pltpu.CompilerParams(
            collective_id=0, has_side_effects=True, vmem_limit_bytes=67043328
        ),
    )(frames, inverse_taps, mode_rate, frame_factor, bt, bp)


def solution(mesh):
    return jax.shard_map(
        on_device,
        mesh=mesh,
        in_specs=(P(("grp", "tm"), "tile", None), P(), P(None, "tile"), P(("grp", "tm"))),
        out_specs=P(("grp", "tm"), "tile", None),
        check_vma=False,
    )
```

time: 605 us -> 257 us (0.42)
  the two profiles are of different devices: /device:TPU:1 before, /device:TPU:31 now
where the time goes in v1:
time: 257 us
  Pallas kernels  219 us (85%)
  other arithmetic  33.4 us (13%)
  local copies, waits for them, and re-layouts  4.64 us (2%)
    pallas_call x1, Pallas kernels, on_device(): pl.pallas_call(kernel, out_shape=jax.ShapeDtypeStruct(frames.shape, b16),...  219 us
    convert_element_type x1, other arithmetic, cosine_values(): return values.astype(jnp.bfloat16)  33.4 us

profile of v1, /device:TPU:31, one launch (start us, length us, event | category | flops | bytes accessed | tf_op | source)
XLA Modules:
  0.0 257.1 jit_solution(11331165467932650137)
XLA Ops:
  0.0 33.4 %select_convert_fusion = (bf16[1024,1024]{1,0:T(8,128)(2,1)}, bf16[1024,1024]{1,0:T(8,128)(2,1)}) fusion(s32[1024]{0:T(1024)S(1)} %get-tuple-element.7, pred[1024]{0:T(1024)(128)(4,1)S(1)} %iota_compare_fusion, s32[1024]{0:T(1024)S(1)} %get-tuple-element.8), kind=kLoop, calls=%fused_computation.14 | loop fusion | flops 37748736 | bytes 4203520 | tf_op jit(solution)/shard_map/convert_element_type | solution.py:21
  33.4 219.0 %shard_map.46 = bf16[8,256,1024]{2,1,0:T(8,128)(2,1)} custom-call(bf16[8,256,1024]{2,1,0:T(8,128)(2,1)} %x_hbm.1, f32[48]{0:T(128)} %taps.1, f32[1024,256]{1,0:T(8,128)} %rate_hbm.1, f32[8]{0:T(128)} %factor.1, bf16[1024,1024]{1,0:T(8,128)(2,1)} %get-tuple-element.6.bt_hbm, bf16[1024,1024]{1,0:T(8,128)(2,1)} %get-tuple-element.5.bp_hbm), custom_call_target="tpu_custom_call" | custom-call | tf_op jit(solution)/shard_map/pallas_call | solution.py:353
  252.5 4.6 %copy.6 = bf16[8,256,1024]{2,1,0:T(8,128)(2,1)} copy(bf16[8,256,1024]{2,1,0:T(8,128)(2,1)} %shard_map.46) | data formatting | bytes 8388608
  (2 shorter events, 0.0 us)

commit v2 on v1

--- a/solution.py
+++ b/solution.py
@@ -1,7 +1,6 @@
-import functools
-
 import jax
 import jax.numpy as jnp
+import numpy as np
 from jax import lax
 from jax.experimental import pallas as pl
 from jax.experimental.pallas import tpu as pltpu
@@ -9,16 +8,17 @@
 
 MESH = pl.DeviceIdType.MESH
 GROUP = 16
-PIECE = 64
+PIECE = 32
+RUN = 2
 CARRY_PIECES = 4
 
 
-def cosine_values(freq_idx, cell_idx, points):
-    phase = (2 * cell_idx + 1) * freq_idx % (4 * points)
-    angle = jnp.pi * phase.astype(jnp.float32) / (2.0 * points)
-    values = jnp.cos(angle) * jnp.sqrt(2.0 / points)
-    values = jnp.where(freq_idx == 0, values / jnp.sqrt(2.0), values)
-    return values.astype(jnp.bfloat16)
+def cosine_table(points):
+    freq_idx = np.arange(points)[None, :]
+    phase = (2 * np.arange(points)[:, None] + 1) * freq_idx % (4 * points)
+    values = np.cos(np.pi * phase / (2.0 * points)) * np.sqrt(2.0 / points)
+    values = np.where(freq_idx == 0, values / np.sqrt(2.0), values)
+    return values.astype(np.float32).astype(jnp.bfloat16)
 
 
 def dot(a, b):
@@ -26,14 +26,15 @@
 
 
 def kernel(
-    x_hbm, taps, rate_hbm, factor, bt_hbm, bp_hbm, out_hbm,
+    x_hbm, taps, rate_hbm, factor, bt_hbm, out_hbm,
     x, hist, bt, bp, retain, flux, send1, colp, acc, tk, carry, cout, dec, rb, send2, rowp, outv,
     load_sem, hist_send, hist_recv, fwd_send, fwd_recv, carry_send, carry_recv,
     inv_send, inv_recv, out_sem,
 ):
     span, rows, side = x.shape
     hops = hist.shape[0]
-    pieces, _, depth, cols = colp.shape
+    runs, _, depth, cols = colp.shape
+    pieces = runs * RUN
     tap_count = taps.shape[0]
     tiles = side // rows
     times = lax.axis_size("tm")
@@ -48,7 +49,7 @@
 
     loads = [
         pltpu.make_async_copy(src, dst, load_sem.at[n])
-        for n, (src, dst) in enumerate(((x_hbm, x), (bt_hbm, bt), (bp_hbm, bp), (rate_hbm, retain)))
+        for n, (src, dst) in enumerate(((x_hbm, x), (bt_hbm, bt), (rate_hbm, retain)))
     ]
     for load in loads:
         load.start()
@@ -64,6 +65,10 @@
 
     def piece_rows(i):
         return pl.ds(pl.multiple_of(i * PIECE, PIECE), PIECE)
+
+    def landing(i, owner):
+        offset = lax.rem(i, RUN) * (depth // RUN) + owner * PIECE
+        return colp.at[i // RUN, :, pl.ds(pl.multiple_of(offset, PIECE), PIECE), :]
 
     def hist_copy(h, i):
         src = x_hbm if h == 0 else hist.at[h - 1]
@@ -82,7 +87,7 @@
     def fwd_copy(i, d):
         return pltpu.make_async_remote_copy(
             src_ref=send1.at[i, d - 1],
-            dst_ref=colp.at[i, :, pl.ds(pl.multiple_of(z * PIECE, PIECE), PIECE), :],
+            dst_ref=landing(i, z),
             send_sem=fwd_send.at[i, d - 1],
             recv_sem=fwd_recv.at[i, d - 1],
             device_id={"tile": partner(d)},
@@ -92,7 +97,7 @@
     def fwd_arrival(i, d):
         return pltpu.make_async_remote_copy(
             src_ref=send1.at[i, d - 1],
-            dst_ref=colp.at[i, :, pl.ds(pl.multiple_of(source(d) * PIECE, PIECE), PIECE), :],
+            dst_ref=landing(i, source(d)),
             send_sem=fwd_send.at[i, d - 1],
             recv_sem=fwd_recv.at[i, d - 1],
             device_id={"tile": partner(d)},
@@ -140,16 +145,22 @@
     for load in loads:
         load.wait()
 
-    def row_transform(i):
-        for d in range(1, tiles):
-            fwd_arrival(i, d).wait_recv()
+    def row_transform(n):
+        pixels = [
+            bt[pl.ds(pl.multiple_of(owner * rows + (n * RUN + part) * PIECE, PIECE), PIECE), :]
+            for part in range(RUN)
+            for owner in range(tiles)
+        ]
+        bp[...] = jnp.concatenate(pixels, axis=0).T
+        for part in range(RUN):
+            for d in range(1, tiles):
+                fwd_arrival(n * RUN + part, d).wait_recv()
 
         def frame(s, _):
-            block = colp[i, s]
+            block = colp[n, s]
             for m in range(side // 256):
                 here = slice(m * 256, (m + 1) * 256)
-                basis = bp[here, pl.ds(pl.multiple_of(i * depth, depth), depth)]
-                acc[s, here, :] += dot(basis, block)
+                acc[s, here, :] += dot(bp[here, :], block)
             return 0
 
         lax.fori_loop(0, span, frame, 0)
@@ -188,14 +199,14 @@
             result = dot(flux[...].reshape(span * PIECE, side), bt[:, modes]).astype(jnp.bfloat16)
             result = result.reshape(span, PIECE, cols)
             if d == 0:
-                colp[i, :, pl.ds(pl.multiple_of(z * PIECE, PIECE), PIECE), :] = result
+                landing(i, z)[...] = result
             else:
                 send1[i, d - 1] = result
                 fwd_copy(i, d).start()
 
-        @pl.when(i > 0)
+        @pl.when(jnp.logical_and(lax.rem(i, RUN) == RUN - 1, i >= RUN))
         def _():
-            row_transform(i - 1)
+            row_transform(i // RUN - 1)
 
         return 0
 
@@ -206,7 +217,7 @@
 
     lax.fori_loop(0, side // 64, decay, 0)
     lax.fori_loop(0, pieces, forward, 0)
-    row_transform(pieces - 1)
+    row_transform(runs - 1)
 
     def close(n, _):
         here = pl.ds(pl.multiple_of(n * 64, 64), 64)
@@ -339,13 +350,9 @@
     tiles = side // rows
     cols = side // tiles
     pieces = rows // PIECE
-    depth = tiles * PIECE
+    depth = tiles * PIECE * RUN
     hops = min((tap_count - 1 + span - 1) // span, lax.axis_size("tm") - 1)
-    index = jnp.arange(side, dtype=jnp.int32)
-    place = index % depth
-    cell = place // PIECE * rows + index // depth * PIECE + place % PIECE
-    bt = cosine_values(index[None, :], index[:, None], side)
-    bp = cosine_values(index[:, None], cell[None, :], side)
+    bt = jnp.asarray(cosine_table(side))
     any_space = pl.BlockSpec(memory_space=pl.ANY)
     smem = pl.BlockSpec(memory_space=pltpu.SMEM)
     b16, f32 = jnp.bfloat16, jnp.float32
@@ -353,17 +360,17 @@
     return pl.pallas_call(
         kernel,
         out_shape=jax.ShapeDtypeStruct(frames.shape, b16),
-        in_specs=[any_space, smem, any_space, smem, any_space, any_space],
+        in_specs=[any_space, smem, any_space, smem, any_space],
         out_specs=any_space,
         scratch_shapes=[
             pltpu.VMEM((span, rows, side), b16),
             pltpu.VMEM((hops, span, rows, side), b16),
             pltpu.VMEM((side, side), b16),
-            pltpu.VMEM((side, side), b16),
+            pltpu.VMEM((side, depth), b16),
             pltpu.VMEM((side, cols), f32),
             pltpu.VMEM((span, PIECE, side), b16),
             pltpu.VMEM((pieces, tiles - 1, span, PIECE, cols), b16),
-            pltpu.VMEM((pieces, span, depth, cols), b16),
+            pltpu.VMEM((pieces // RUN, span, depth, cols), b16),
             pltpu.VMEM((span, side, cols), f32),
             pltpu.VMEM((span * GROUP, (hops + 1) * span * GROUP), f32),
             pltpu.VMEM((side, cols), f32),
@@ -373,7 +380,7 @@
             pltpu.VMEM((span, tiles - 1, rows, cols), b16),
             pltpu.VMEM((span, rows, side), b16),
             pltpu.VMEM((span, rows, side), b16),
-            dma((4,)),
+            dma((3,)),
             dma((hops, pieces)),
             dma((hops, pieces)),
             dma((pieces, tiles - 1)),
@@ -387,7 +394,7 @@
         compiler_params=pltpu.CompilerParams(
             collective_id=0, has_side_effects=True, vmem_limit_bytes=67043328
         ),
-    )(frames, inverse_taps, mode_rate, frame_factor, bt, bp)
+    )(frames, inverse_taps, mode_rate, frame_factor, bt)
 
 
 def solution(mesh):

time: 257 us -> 217 us (0.84)
  other arithmetic: 33.4 us -> 0 us
  Pallas kernels: 219 us -> 212 us
    convert_element_type x1 -> x0, other arithmetic: 33.4 us -> none  [cosine_values(): return values.astype(jnp.bfloat16)]
    pallas_call x1, Pallas kernels: 219 us -> 212 us  [on_device(): pl.pallas_call(kernel, out_shape=jax.ShapeDtypeStruct(frames.shape, b16),...]
where the time goes in v2:
time: 217 us
  Pallas kernels  212 us (98%)
  local copies, waits for them, and re-layouts  4.64 us (2%)
    pallas_call x1, Pallas kernels, on_device(): pl.pallas_call(kernel, out_shape=jax.ShapeDtypeStruct(frames.shape, b16),...  212 us
    unnamed x1, local copies, waits for them, and re-layouts  4.64 us

profile of v2, /device:TPU:31, one launch (start us, length us, event | category | flops | bytes accessed | tf_op | source)
XLA Modules:
  0.0 216.8 jit_solution(3398947721899961728)
XLA Ops:
  0.0 212.2 %shard_map.55 = bf16[8,256,1024]{2,1,0:T(8,128)(2,1)} custom-call(bf16[8,256,1024]{2,1,0:T(8,128)(2,1)} %x_hbm.1, f32[48]{0:T(128)} %taps.1, f32[1024,256]{1,0:T(8,128)} %rate_hbm.1, f32[8]{0:T(128)} %factor.1, bf16[1024,1024]{1,0:T(8,128)(2,1)} %constant.2.clone.bt_hbm), custom_call_target="tpu_custom_call" | custom-call | tf_op jit(solution)/shard_map/pallas_call | solution.py:360
  212.2 4.6 %copy.7 = bf16[8,256,1024]{2,1,0:T(8,128)(2,1)} copy(bf16[8,256,1024]{2,1,0:T(8,128)(2,1)} %shard_map.55) | data formatting | bytes 8388608

commit v3 on v2

--- a/solution.py
+++ b/solution.py
@@ -27,7 +27,7 @@
 
 def kernel(
     x_hbm, taps, rate_hbm, factor, bt_hbm, out_hbm,
-    x, hist, bt, bp, retain, flux, send1, colp, acc, tk, carry, cout, dec, rb, send2, rowp, outv,
+    x, hist, bt, bp, retain, flux, send1, colp, acc, tk, carry, cout, dec, rb, send2, rowp,
     load_sem, hist_send, hist_recv, fwd_send, fwd_recv, carry_send, carry_recv,
     inv_send, inv_recv, out_sem,
 ):
@@ -126,26 +126,10 @@
 
     lax.fori_loop(0, span, tap_rows, 0)
 
-    for h in range(hops):
-
-        @pl.when(j <= h)
-        def _(h=h):
-            def clear(s, _):
-                hist[h, s] = jnp.zeros((rows, side), hist.dtype)
-                return 0
-
-            lax.fori_loop(0, span, clear, 0)
-
-    def clear_acc(s, _):
-        acc[s] = jnp.zeros((side, cols), jnp.float32)
-        return 0
-
-    lax.fori_loop(0, span, clear_acc, 0)
-
-    for load in loads:
-        load.wait()
-
-    def row_transform(n):
+    loads[0].wait()
+    loads[1].wait()
+
+    def row_setup(n):
         pixels = [
             bt[pl.ds(pl.multiple_of(owner * rows + (n * RUN + part) * PIECE, PIECE), PIECE), :]
             for part in range(RUN)
@@ -156,14 +140,21 @@
             for d in range(1, tiles):
                 fwd_arrival(n * RUN + part, d).wait_recv()
 
+    def row_frames(n, first, start):
         def frame(s, _):
             block = colp[n, s]
             for m in range(side // 256):
                 here = slice(m * 256, (m + 1) * 256)
-                acc[s, here, :] += dot(bp[here, :], block)
+                share = dot(bp[here, :], block)
+                acc[s, here, :] = share if first else acc[s, here, :] + share
             return 0
 
-        lax.fori_loop(0, span, frame, 0)
+        lax.fori_loop(start, span, frame, 0)
+
+    def decay(n, _):
+        here = pl.ds(pl.multiple_of(n * 64, 64), 64)
+        retain[here, :] = jnp.exp(-retain[here, :])
+        return 0
 
     def forward(i, _):
         for h in range(hops):
@@ -171,6 +162,10 @@
             @pl.when(j > h)
             def _(h=h):
                 hist_copy(h, i).wait_recv()
+
+            @pl.when(j <= h)
+            def _(h=h):
+                hist[h, :, piece_rows(i), :] = jnp.zeros((span, PIECE, side), hist.dtype)
 
             if h + 1 < hops:
 
@@ -206,18 +201,26 @@
 
         @pl.when(jnp.logical_and(lax.rem(i, RUN) == RUN - 1, i >= RUN))
         def _():
-            row_transform(i // RUN - 1)
-
-        return 0
-
-    def decay(n, _):
-        here = pl.ds(pl.multiple_of(n * 64, 64), 64)
-        retain[here, :] = jnp.exp(-retain[here, :])
-        return 0
-
-    lax.fori_loop(0, side // 64, decay, 0)
+            n = i // RUN - 1
+            row_setup(n)
+
+            @pl.when(n == 0)
+            def _():
+                row_frames(n, True, 0)
+
+            @pl.when(n > 0)
+            def _():
+                row_frames(n, False, 0)
+
+        @pl.when(i == pieces - 1)
+        def _():
+            loads[2].wait()
+            lax.fori_loop(0, side // 64, decay, 0)
+
+        return 0
+
     lax.fori_loop(0, pieces, forward, 0)
-    row_transform(runs - 1)
+    row_setup(runs - 1)
 
     def close(n, _):
         here = pl.ds(pl.multiple_of(n * 64, 64), 64)
@@ -232,7 +235,14 @@
         dec[here, :] = whole
         return 0
 
-    lax.fori_loop(0, side // 64, close, 0)
+    def close_exact(n, _):
+        here = pl.ds(pl.multiple_of(n * 64, 64), 64)
+        rate = retain[here, :]
+        last = carry[here, :]
+        for s in range(1, span):
+            last = (rate * factor[s]) * last + acc[s, here, :]
+        cout[here, :] = last
+        return 0
 
     share = side // CARRY_PIECES
 
@@ -246,22 +256,6 @@
             device_id={"tm": lax.rem(j + 1, times)},
             device_id_type=MESH,
         )
-
-    @pl.when(j == 0)
-    def _():
-        carry[...] = jnp.zeros_like(carry)
-
-    for q in range(CARRY_PIECES):
-
-        @pl.when(j > 0)
-        def _(q=q):
-            carry_copy(q).wait_recv()
-            here = pl.ds(q * share, share)
-            cout[here, :] = dec[here, :] * carry[here, :] + cout[here, :]
-
-        @pl.when(j < times - 1)
-        def _(q=q):
-            carry_copy(q).start()
 
     def inv_copy(s, d):
         return pltpu.make_async_remote_copy(
@@ -304,15 +298,59 @@
                 inv_copy(s, d).start()
         return 0
 
-    lax.fori_loop(0, span, inverse, 0)
+    early = lax.rem(j, 2) == 0
+    last_first = runs == 1
+
+    @pl.when(early)
+    def _():
+        @pl.when(j == 0)
+        def _():
+            carry[...] = jnp.zeros_like(carry)
+
+        row_frame_0 = colp[runs - 1, 0]
+        for m in range(side // 256):
+            here = slice(m * 256, (m + 1) * 256)
+            part = dot(bp[here, :], row_frame_0)
+            acc[0, here, :] = part if last_first else acc[0, here, :] + part
+
+        @pl.when(j > 0)
+        def _():
+            for q in range(CARRY_PIECES):
+                carry_copy(q).wait_recv()
+
+        inverse(0, 0)
+        row_frames(runs - 1, last_first, 1)
+        for q in range(CARRY_PIECES):
+            lax.fori_loop(q * share // 64, (q + 1) * share // 64, close_exact, 0)
+
+            @pl.when(j < times - 1)
+            def _(q=q):
+                carry_copy(q).start()
+
+        lax.fori_loop(1, span, inverse, 0)
+
+    @pl.when(jnp.logical_not(early))
+    def _():
+        row_frames(runs - 1, last_first, 0)
+        lax.fori_loop(0, side // 64, close, 0)
+        for q in range(CARRY_PIECES):
+            carry_copy(q).wait_recv()
+            here = pl.ds(q * share, share)
+            cout[here, :] = dec[here, :] * carry[here, :] + cout[here, :]
+
+            @pl.when(j < times - 1)
+            def _(q=q):
+                carry_copy(q).start()
+
+        lax.fori_loop(0, span, inverse, 0)
 
     def finish(s, _):
         for d in range(1, tiles):
             inv_arrival(s, d).wait_recv()
-        outv[s] = lax.dot_general(
+        x[s] = lax.dot_general(
             rowp[s], bt[...], (((1,), (1,)), ((), ())), preferred_element_type=jnp.float32
         ).astype(jnp.bfloat16)
-        pltpu.make_async_copy(outv.at[s], out_hbm.at[s], out_sem.at[s]).start()
+        pltpu.make_async_copy(x.at[s], out_hbm.at[s], out_sem.at[s]).start()
         return 0
 
     lax.fori_loop(0, span, finish, 0)
@@ -320,7 +358,7 @@
     def drain_frames(s, _):
         for d in range(1, tiles):
             inv_copy(s, d).wait_send()
-        pltpu.make_async_copy(outv.at[s], out_hbm.at[s], out_sem.at[s]).wait()
+        pltpu.make_async_copy(x.at[s], out_hbm.at[s], out_sem.at[s]).wait()
         return 0
 
     lax.fori_loop(0, span, drain_frames, 0)
@@ -379,7 +417,6 @@
             pltpu.VMEM((side, cols), b16),
             pltpu.VMEM((span, tiles - 1, rows, cols), b16),
             pltpu.VMEM((span, rows, side), b16),
-            pltpu.VMEM((span, rows, side), b16),
             dma((3,)),
             dma((hops, pieces)),
             dma((hops, pieces)),

time: 217 us -> 217 us (level)
  no operation moved by 1% of the time
where the time goes in v3:
time: 217 us
  Pallas kernels  212 us (98%)
  local copies, waits for them, and re-layouts  4.64 us (2%)
    pallas_call x1, Pallas kernels, on_device(): pl.pallas_call(kernel, out_shape=jax.ShapeDtypeStruct(frames.shape, b16),...  212 us
    unnamed x1, local copies, waits for them, and re-layouts  4.64 us

profile of v3, /device:TPU:31, one launch (start us, length us, event | category | flops | bytes accessed | tf_op | source)
XLA Modules:
  0.0 216.7 jit_solution(5337548168664902129)
XLA Ops:
  0.0 212.0 %shard_map.55 = bf16[8,256,1024]{2,1,0:T(8,128)(2,1)} custom-call(bf16[8,256,1024]{2,1,0:T(8,128)(2,1)} %x_hbm.1, f32[48]{0:T(128)} %taps.1, f32[1024,256]{1,0:T(8,128)} %rate_hbm.1, f32[8]{0:T(128)} %factor.1, bf16[1024,1024]{1,0:T(8,128)(2,1)} %constant.2.clone.bt_hbm), custom_call_target="tpu_custom_call" | custom-call | tf_op jit(solution)/shard_map/pallas_call | solution.py:398
  212.0 4.6 %copy.7 = bf16[8,256,1024]{2,1,0:T(8,128)(2,1)} copy(bf16[8,256,1024]{2,1,0:T(8,128)(2,1)} %shard_map.55) | data formatting | bytes 8388608

commit v4 on v3

--- a/solution.py
+++ b/solution.py
@@ -27,7 +27,7 @@
 
 def kernel(
     x_hbm, taps, rate_hbm, factor, bt_hbm, out_hbm,
-    x, hist, bt, bp, retain, flux, send1, colp, acc, tk, carry, cout, dec, rb, send2, rowp,
+    x, hist, bt, bp, retain, flux, send1, colp, acc, tk, carry, came, cout, dec, rb, send2, rowp,
     load_sem, hist_send, hist_recv, fwd_send, fwd_recv, carry_send, carry_recv,
     inv_send, inv_recv, out_sem,
 ):
@@ -231,8 +231,20 @@
             now = rate * factor[s]
             last = now * last + acc[s, here, :]
             whole = now * whole
-        cout[here, :] = last
+        carry[here, :] = last
         dec[here, :] = whole
+        return 0
+
+    def join(n, _):
+        here = pl.ds(pl.multiple_of(n * 64, 64), 64)
+        state = came[here, :].astype(jnp.float32)
+        cout[here, :] = (dec[here, :] * state + carry[here, :]).astype(jnp.bfloat16)
+        carry[here, :] = state
+        return 0
+
+    def open_state(n, _):
+        here = pl.ds(pl.multiple_of(n * 64, 64), 64)
+        carry[here, :] = came[here, :].astype(jnp.float32)
         return 0
 
     def close_exact(n, _):
@@ -241,7 +253,7 @@
         last = carry[here, :]
         for s in range(1, span):
             last = (rate * factor[s]) * last + acc[s, here, :]
-        cout[here, :] = last
+        cout[here, :] = last.astype(jnp.bfloat16)
         return 0
 
     share = side // CARRY_PIECES
@@ -250,7 +262,7 @@
         here = pl.ds(q * share, share)
         return pltpu.make_async_remote_copy(
             src_ref=cout.at[here, :],
-            dst_ref=carry.at[here, :],
+            dst_ref=came.at[here, :],
             send_sem=carry_send.at[q],
             recv_sem=carry_recv.at[q],
             device_id={"tm": lax.rem(j + 1, times)},
@@ -298,30 +310,27 @@
                 inv_copy(s, d).start()
         return 0
 
-    early = lax.rem(j, 2) == 0
+    def quarter(q, body):
+        lax.fori_loop(q * share // 64, (q + 1) * share // 64, body, 0)
+
+    early = jnp.logical_and(lax.rem(j, 2) == 0, j > 0)
     last_first = runs == 1
 
     @pl.when(early)
     def _():
-        @pl.when(j == 0)
-        def _():
-            carry[...] = jnp.zeros_like(carry)
-
-        row_frame_0 = colp[runs - 1, 0]
+        first_frame = colp[runs - 1, 0]
         for m in range(side // 256):
             here = slice(m * 256, (m + 1) * 256)
-            part = dot(bp[here, :], row_frame_0)
+            part = dot(bp[here, :], first_frame)
             acc[0, here, :] = part if last_first else acc[0, here, :] + part
-
-        @pl.when(j > 0)
-        def _():
-            for q in range(CARRY_PIECES):
-                carry_copy(q).wait_recv()
+        for q in range(CARRY_PIECES):
+            carry_copy(q).wait_recv()
+            quarter(q, open_state)
 
         inverse(0, 0)
         row_frames(runs - 1, last_first, 1)
         for q in range(CARRY_PIECES):
-            lax.fori_loop(q * share // 64, (q + 1) * share // 64, close_exact, 0)
+            quarter(q, close_exact)
 
             @pl.when(j < times - 1)
             def _(q=q):
@@ -332,11 +341,19 @@
     @pl.when(jnp.logical_not(early))
     def _():
         row_frames(runs - 1, last_first, 0)
-        lax.fori_loop(0, side // 64, close, 0)
+
+        @pl.when(j == 0)
+        def _():
+            came[...] = jnp.zeros_like(came)
+
         for q in range(CARRY_PIECES):
-            carry_copy(q).wait_recv()
-            here = pl.ds(q * share, share)
-            cout[here, :] = dec[here, :] * carry[here, :] + cout[here, :]
+            quarter(q, close)
+
+            @pl.when(j > 0)
+            def _(q=q):
+                carry_copy(q).wait_recv()
+
+            quarter(q, join)
 
             @pl.when(j < times - 1)
             def _(q=q):
@@ -412,7 +429,8 @@
             pltpu.VMEM((span, side, cols), f32),
             pltpu.VMEM((span * GROUP, (hops + 1) * span * GROUP), f32),
             pltpu.VMEM((side, cols), f32),
-            pltpu.VMEM((side, cols), f32),
+            pltpu.VMEM((side, cols), b16),
+            pltpu.VMEM((side, cols), b16),
             pltpu.VMEM((side, cols), f32),
             pltpu.VMEM((side, cols), b16),
             pltpu.VMEM((span, tiles - 1, rows, cols), b16),

time: 217 us -> 210 us (0.968)
  Pallas kernels: 212 us -> 205 us
    pallas_call x1, Pallas kernels: 212 us -> 205 us  [on_device(): pl.pallas_call(kernel, out_shape=jax.ShapeDtypeStruct(frames.shape, b16),...]
where the time goes in v4:
time: 210 us
  Pallas kernels  205 us (98%)
  local copies, waits for them, and re-layouts  4.64 us (2%)
    pallas_call x1, Pallas kernels, on_device(): pl.pallas_call(kernel, out_shape=jax.ShapeDtypeStruct(frames.shape, b16),...  205 us
    unnamed x1, local copies, waits for them, and re-layouts  4.64 us

profile of v4, /device:TPU:31, one launch (start us, length us, event | category | flops | bytes accessed | tf_op | source)
XLA Modules:
  0.0 209.8 jit_solution(10257720348985309260)
XLA Ops:
  0.0 205.1 %shard_map.55 = bf16[8,256,1024]{2,1,0:T(8,128)(2,1)} custom-call(bf16[8,256,1024]{2,1,0:T(8,128)(2,1)} %x_hbm.1, f32[48]{0:T(128)} %taps.1, f32[1024,256]{1,0:T(8,128)} %rate_hbm.1, f32[8]{0:T(128)} %factor.1, bf16[1024,1024]{1,0:T(8,128)(2,1)} %constant.2.clone.bt_hbm), custom_call_target="tpu_custom_call" | custom-call | tf_op jit(solution)/shard_map/pallas_call | solution.py:415
  205.1 4.6 %copy.7 = bf16[8,256,1024]{2,1,0:T(8,128)(2,1)} copy(bf16[8,256,1024]{2,1,0:T(8,128)(2,1)} %shard_map.55) | data formatting | bytes 8388608

commit v5 on v4

--- a/solution.py
+++ b/solution.py
@@ -8,8 +8,8 @@
 
 MESH = pl.DeviceIdType.MESH
 GROUP = 16
-PIECE = 32
-RUN = 2
+PIECE = 16
+RUN = 4
 CARRY_PIECES = 4
 
 

time: 210 us -> 210 us (level)
  no operation moved by 1% of the time
where the time goes in v5:
time: 210 us
  Pallas kernels  205 us (98%)
  local copies, waits for them, and re-layouts  4.64 us (2%)
    pallas_call x1, Pallas kernels, on_device(): pl.pallas_call(kernel, out_shape=jax.ShapeDtypeStruct(frames.shape, b16),...  205 us
    unnamed x1, local copies, waits for them, and re-layouts  4.64 us

profile of v5, /device:TPU:31, one launch (start us, length us, event | category | flops | bytes accessed | tf_op | source)
XLA Modules:
  0.0 209.5 jit_solution(17725855175220894984)
XLA Ops:
  0.0 204.9 %shard_map.55 = bf16[8,256,1024]{2,1,0:T(8,128)(2,1)} custom-call(bf16[8,256,1024]{2,1,0:T(8,128)(2,1)} %x_hbm.1, f32[48]{0:T(128)} %taps.1, f32[1024,256]{1,0:T(8,128)} %rate_hbm.1, f32[8]{0:T(128)} %factor.1, bf16[1024,1024]{1,0:T(8,128)(2,1)} %constant.2.clone.bt_hbm), custom_call_target="tpu_custom_call" | custom-call | tf_op jit(solution)/shard_map/pallas_call | solution.py:415
  204.9 4.6 %copy.7 = bf16[8,256,1024]{2,1,0:T(8,128)(2,1)} copy(bf16[8,256,1024]{2,1,0:T(8,128)(2,1)} %shard_map.55) | data formatting | bytes 8388608

commit v6 on v5

--- a/solution.py
+++ b/solution.py
@@ -189,7 +189,7 @@
 
         lax.fori_loop(0, PIECE // GROUP, group, 0)
 
-        for d in list(range(1, tiles)) + [0]:
+        for d in sorted(range(1, tiles), key=lambda d: abs(2 * d - tiles)) + [0]:
             modes = pl.ds(pl.multiple_of(partner(d) * cols, cols), cols)
             result = dot(flux[...].reshape(span * PIECE, side), bt[:, modes]).astype(jnp.bfloat16)
             result = result.reshape(span, PIECE, cols)
@@ -300,7 +300,7 @@
             return 0
 
         lax.fori_loop(0, side // 128, advance, 0)
-        for d in list(range(1, tiles)) + [0]:
+        for d in sorted(range(1, tiles), key=lambda d: abs(2 * d - tiles)) + [0]:
             mine = pl.ds(pl.multiple_of(partner(d) * rows, rows), rows)
             result = dot(bt[mine, :], rb[...]).astype(jnp.bfloat16)
             if d == 0:

time: 210 us -> 210 us (level)
  no operation moved by 1% of the time
where the time goes in v6:
time: 210 us; the launch traced here: 208 us
  Pallas kernels  203 us (97%)
  local copies, waits for them, and re-layouts  4.64 us (2%)
    pallas_call x1, Pallas kernels, on_device(): pl.pallas_call(kernel, out_shape=jax.ShapeDtypeStruct(frames.shape, b16),...  203 us
    unnamed x1, local copies, waits for them, and re-layouts  4.64 us

profile of v6, /device:TPU:31, one launch (start us, length us, event | category | flops | bytes accessed | tf_op | source)
XLA Modules:
  0.0 207.6 jit_solution(12926133884181936743)
XLA Ops:
  0.0 203.0 %shard_map.55 = bf16[8,256,1024]{2,1,0:T(8,128)(2,1)} custom-call(bf16[8,256,1024]{2,1,0:T(8,128)(2,1)} %x_hbm.1, f32[48]{0:T(128)} %taps.1, f32[1024,256]{1,0:T(8,128)} %rate_hbm.1, f32[8]{0:T(128)} %factor.1, bf16[1024,1024]{1,0:T(8,128)(2,1)} %constant.2.clone.bt_hbm), custom_call_target="tpu_custom_call" | custom-call | tf_op jit(solution)/shard_map/pallas_call | solution.py:415
  203.0 4.6 %copy.7 = bf16[8,256,1024]{2,1,0:T(8,128)(2,1)} copy(bf16[8,256,1024]{2,1,0:T(8,128)(2,1)} %shard_map.55) | data formatting | bytes 8388608
